TPU v7x, 32 devices: a whole 2x2x4 slice. The times are simulated.
32 devices in a mesh: row: 8 (over y, x, core), col: 4 (over z).
Axes of the slice: x: 2, y: 2, z: 4, core: 2. Of those that a mesh axis runs over, the one named last changes fastest.
Arguments:
- stored_blocks: bfloat16 [8, 4, 64, 128, 128], P('row', 'col'), may hold values from -1 to 1
- stored_ids: int32 [8, 4, 3, 64], P('row', 'col'), may hold values from 0 to 127, as said below
- slab_blocks: bfloat16 [8, 4, 32, 128, 128], P('row', 'col'), may hold values from -1 to 1
- slab_ids: int32 [8, 4, 3, 32], P('row', 'col'), may hold values from 0 to 127, as said below
- pair_lists: int32 [8, 4, 4, 3, 256], P('row', 'col'), may hold values from 0 to 127, as said below
Outputs:
- product: bfloat16 [16384, 1024], P('row', 'col')
Inputs may be any that keep to these rules, and one draw needn't show every extreme that they name: `stored_ids`: present slots of cell (r, c) hold blocks of the panel pair made of panels r and r xor c: row index in the lower of the two panels (panel p covers block rows p * 16 to (p + 1) * 16 - 1), column index in the higher, row <= column. Every stored block lies in exactly one slot over all cells. Flags are 0 or 1; a half has at most 64 present slots and some halves have exactly 64. `slab_ids`: the slots of cell (r, c) name each block of panel r xor c and slab columns c * 2 to (c + 1) * 2 - 1 exactly once; flags are 0 or 1, and some cells have all flags 1. pair_lists[r, c, s] names, with flag 1 and ahead of every entry with flag 0, each pair of a present entry of A_s and a present entry of B_s whose column index and row index agree, once each; some list has all 256 flags 1.
All inputs are finite; a program needn't handle non-finite values.
Results may differ from a plain program's by a relative error of at most 0.001.
Values may be sent and summed in bfloat16 or wider, within the bound.
A program may use at most 128 MiB of HBM per device.

v0:
```python
import jax
import jax.numpy as jnp
from jax import lax
from jax.sharding import PartitionSpec as P

PANEL = 16
SLAB = 2
STEPS = 4


def swapped(value, axis, apart):
    mask = 2**apart
    pairs = [(source, source ^ mask) for source in range(lax.axis_size(axis))]
    return lax.ppermute(value, axis, pairs)


def orient(values, block_ids, transpose, drop_diag):
    turned = lax.cond(
        transpose, lambda blocks: jnp.swapaxes(blocks, 1, 2), lambda blocks: blocks, values
    )
    row_ids = jnp.where(transpose, block_ids[1], block_ids[0])
    present = block_ids[2]
    if drop_diag:
        present = present * (block_ids[0] != block_ids[1]).astype(jnp.int32)
    return (turned, jnp.stack([row_ids, present]))


def gray_offset(step_index):
    return step_index ^ step_index >> 1


def multiply(summed, left_all, left_ids, right_all, right_ids, listed, out_row, out_col):
    cell_count = PANEL * SLAB
    group_size = min(listed.shape[1], 128)

    def add_group(group_index, running):
        pair_group = lax.dynamic_slice_in_dim(listed, group_index * group_size, group_size, 1)
        left_slot = pair_group[0]
        right_slot = pair_group[1]
        weights = pair_group[2] * left_ids[1][left_slot] * right_ids[1][right_slot]
        target = (
            (left_ids[0][left_slot] - out_row * PANEL) * SLAB
            + right_ids[0][right_slot]
            - out_col * SLAB
        )
        target = jnp.where(weights > 0, target, cell_count)
        blocks = jnp.einsum(
            "pij,pjk->pik",
            left_all[left_slot],
            right_all[right_slot],
            preferred_element_type=jnp.float32,
        )
        return (
            running + jax.ops.segment_sum(blocks, target, num_segments=cell_count + 1)[:cell_count]
        )

    groups = listed.shape[1] // group_size
    return lax.fori_loop(0, groups, add_group, summed)


def on_device(stored_blocks, stored_ids, slab_blocks, slab_ids, pair_lists):
    grid_row = lax.axis_index("row")
    grid_col = lax.axis_index("col")
    stride_len = lax.axis_size("col") // STEPS
    own_blocks = stored_blocks[0, 0]
    own_ids = stored_ids[0, 0]
    edge = own_blocks.shape[-1]
    moved_blocks, moved_ids = (own_blocks, own_ids)
    for bit_index in range(lax.axis_size("col").bit_length() - 1):
        fetched_blocks, fetched_ids = swapped((moved_blocks, moved_ids), "row", bit_index)
        use_partner = jnp.bitwise_and(jnp.right_shift(grid_col, bit_index), 1) == 1
        moved_blocks = jnp.where(use_partner, fetched_blocks, moved_blocks)
        moved_ids = jnp.where(use_partner, fetched_ids, moved_ids)
    panel_index = jnp.bitwise_xor(grid_row, grid_col)
    first_blocks, first_ids = orient(own_blocks, own_ids, grid_row > panel_index, False)
    second_blocks, second_ids = orient(moved_blocks, moved_ids, grid_row >= panel_index, True)
    left_blocks = jnp.concatenate([first_blocks, second_blocks], 0)
    left_ids = jnp.concatenate([first_ids, second_ids], 1)
    right_blocks = slab_blocks[0, 0]
    right_ids = slab_ids[0, 0, 1:]
    lists = pair_lists[0, 0]
    cell_count = PANEL * SLAB
    summed = jnp.zeros((cell_count, edge, edge), jnp.float32)
    previous = 0
    for step_index in range(STEPS):
        gray = gray_offset(step_index)
        offset = gray * stride_len
        if step_index > 0:
            bit_index = (offset ^ previous).bit_length() - 1
            left_blocks, left_ids = swapped((left_blocks, left_ids), "col", bit_index)
            right_blocks, right_ids = swapped((right_blocks, right_ids), "row", bit_index)
        summed = multiply(
            summed, left_blocks, left_ids, right_blocks, right_ids, lists[gray], grid_row, grid_col
        )
        previous = offset
    out_tile = summed.reshape(PANEL, SLAB, edge, edge).transpose(0, 2, 1, 3)
    return out_tile.reshape(PANEL * edge, SLAB * edge).astype(jnp.bfloat16)


def solution(mesh):
    return jax.shard_map(
        on_device,
        mesh=mesh,
        in_specs=(
            P("row", "col", None, None, None),
            P("row", "col", None, None),
            P("row", "col", None, None, None),
            P("row", "col", None, None),
            P("row", "col", None, None, None),
        ),
        out_specs=P("row", "col"),
        check_vma=False,
    )
```

profile of v0, /device:TPU:1, one launch (start us, length us, event | category | flops | bytes accessed | tf_op | source)
XLA Modules:
  0.0 562.6 jit_solution(11445956436515498555)
XLA Ops:
  15.7 66.1 %collective-permute-done.1 = s32[3,64]{1,0:T(4,128)S(1)} collective-permute-done((s32[3,64]{1,0:T(4,128)S(1)}, s32[3,64]{1,0:T(4,128)S(1)}, u32[]{:S(2)}, u32[]{:S(2)}) %collective-permute-start.1) | collective-permute-done | bytes 800 | tf_op jit(solution)/shard_map/ppermute | solution.py:14
  95.0 6.6 %conditional.3 = (bf16[64,128,128]{2,1,0:T(8,128)(2,1)S(1)}) conditional(s32[]{:T(128)} %convert_element_type.20, (pred[]{:T(512)}, bf16[64,128,128]{2,1,0:T(8,128)(2,1)}, bf16[64,128,128]{2,1,0:T(8,128)(2,1)}) %tuple.114, (pred[]{:T(512)}, bf16[64,128,128]{2,1,0:T(8,128)(2,1)}, bf16[64,128,128]{2,1,0:T(8,128)(2,1)}) %tuple.114), branch_computations={%region_2.3_spmd, %region_3.4_spmd} | conditional | flops 1048576 | bytes 10485769 | solution.py:18
  104.5 82.3 %while.64 = (s32[]{:T(128)}, f32[32,128,128]{2,1,0:T(8,128)}, s32[3,256]{1,0:T(4,128)S(1)}, s32[2,128]{1,0:T(2,128)S(1)}, s32[2,32]{1,0:T(2,128)S(1)}, /*index=5...) while((s32[]{:T(128)}, f32[32,128,128]{2,1,0:T(8,128)}, ...), condition=%wide.region_6.7_spmd.clone, body=%wide.region_4.6_spmd.clone.sunk | while | flops 540020480 | bytes 67202248 | solution.py:58
  112.9 8.0 %fusion.65 = f32[128,128,128]{2,1,0:T(8,128)} fusion(bf16[128,128,128]{2,1,0:T(8,128)(2,1)} %gather_fusion.22, bf16[128,128,128]{2,1,0:T(8,128)(2,1)} %gather_fusion.23), kind=kOutput, calls=%fused_computation.115.clone.1 | convolution fusion | flops 536870912 | bytes 16777216 | tf_op jit(solution)/shard_map/while/body/eval_jaxpr/pij,pjk->pik/dot_general | solution.py:47
  126.1 17.1 %scatter_fusion.3 = f32[33,128,128]{2,1,0:T(8,128)S(1)} fusion(f32[33,128,128]{2,1,0:T(8,128)S(1)} %broadcast.722, s32[128]{0:T(128)S(1)} %fusion.64, f32[128,128,128]{2,1,0:T(8,128)} %fusion.65), kind=kCustom, calls=%fused_computation.24.clone.clone.1 | custom fusion | flops 2097152 | bytes 25166336 | tf_op jit(solution)/shard_map/while/body/eval_jaxpr/scatter-add | solution.py:54
  153.2 8.0 %fusion.65 = f32[128,128,128]{2,1,0:T(8,128)} fusion(bf16[128,128,128]{2,1,0:T(8,128)(2,1)} %gather_fusion.22, bf16[128,128,128]{2,1,0:T(8,128)(2,1)} %gather_fusion.23), kind=kOutput, calls=%fused_computation.115.clone.1 | convolution fusion | flops 536870912 | bytes 16777216 | tf_op jit(solution)/shard_map/while/body/eval_jaxpr/pij,pjk->pik/dot_general | solution.py:47
  166.5 17.0 %scatter_fusion.3 = f32[33,128,128]{2,1,0:T(8,128)S(1)} fusion(f32[33,128,128]{2,1,0:T(8,128)S(1)} %broadcast.722, s32[128]{0:T(128)S(1)} %fusion.64, f32[128,128,128]{2,1,0:T(8,128)} %fusion.65), kind=kCustom, calls=%fused_computation.24.clone.clone.1 | custom fusion | flops 2097152 | bytes 25166336 | tf_op jit(solution)/shard_map/while/body/eval_jaxpr/scatter-add | solution.py:54
  186.8 8.5 %collective-permute-done.6 = bf16[128,128,128]{2,1,0:T(8,128)(2,1)} collective-permute-done((bf16[128,128,128]{2,1,0:T(8,128)(2,1)}, bf16[128,128,128]{2,1,0:T(8,128)(2,1)}, u32[]{:S(2)}, u32[]{:S(2)}) %collective-permute-start.6) | collective-permute-done | bytes 4194336 | tf_op jit(solution)/shard_map/ppermute | solution.py:14
  195.3 84.0 %while.61 = (s32[]{:T(128)}, f32[32,128,128]{2,1,0:T(8,128)}, s32[3,256]{1,0:T(4,128)S(1)}, s32[2,128]{1,0:T(2,128)S(1)}, s32[2,32]{1,0:T(2,128)S(1)}, /*index=5...) while((s32[]{:T(128)}, f32[32,128,128]{2,1,0:T(8,128)}, ...), condition=%wide.region_9.10_spmd, body=%wide.region_7.9_spmd.sunk | while | flops 539496192 | bytes 71396576 | solution.py:58
  203.8 8.0 %fusion.50 = f32[128,128,128]{2,1,0:T(8,128)} fusion(bf16[128,128,128]{2,1,0:T(8,128)(2,1)} %gather_fusion.4, bf16[128,128,128]{2,1,0:T(8,128)(2,1)} %gather_fusion.5), kind=kOutput, calls=%fused_computation.112.clone.1 | convolution fusion | flops 536870912 | bytes 16777216 | tf_op jit(solution)/shard_map/while/body/eval_jaxpr/pij,pjk->pik/dot_general | solution.py:47
  217.1 17.1 %scatter_fusion = f32[33,128,128]{2,1,0:T(8,128)S(1)} fusion(f32[33,128,128]{2,1,0:T(8,128)S(1)} %broadcast.696, s32[128]{0:T(128)S(1)} %fusion.49, f32[128,128,128]{2,1,0:T(8,128)} %fusion.50), kind=kCustom, calls=%fused_computation.25.clone.1 | custom fusion | flops 2097152 | bytes 25166336 | tf_op jit(solution)/shard_map/while/body/eval_jaxpr/scatter-add | solution.py:54
  245.8 8.0 %fusion.50 = f32[128,128,128]{2,1,0:T(8,128)} fusion(bf16[128,128,128]{2,1,0:T(8,128)(2,1)} %gather_fusion.4, bf16[128,128,128]{2,1,0:T(8,128)(2,1)} %gather_fusion.5), kind=kOutput, calls=%fused_computation.112.clone.1 | convolution fusion | flops 536870912 | bytes 16777216 | tf_op jit(solution)/shard_map/while/body/eval_jaxpr/pij,pjk->pik/dot_general | solution.py:47
  259.1 17.1 %scatter_fusion = f32[33,128,128]{2,1,0:T(8,128)S(1)} fusion(f32[33,128,128]{2,1,0:T(8,128)S(1)} %broadcast.696, s32[128]{0:T(128)S(1)} %fusion.49, f32[128,128,128]{2,1,0:T(8,128)} %fusion.50), kind=kCustom, calls=%fused_computation.25.clone.1 | custom fusion | flops 2097152 | bytes 25166336 | tf_op jit(solution)/shard_map/while/body/eval_jaxpr/scatter-add | solution.py:54
  279.3 99.0 %collective-permute-done.10 = bf16[128,128,128]{2,1,0:T(8,128)(2,1)} collective-permute-done((bf16[128,128,128]{2,1,0:T(8,128)(2,1)}, bf16[128,128,128]{2,1,0:T(8,128)(2,1)}, u32[]{:S(2)}, u32[]{:S(2)}) %collective-permute-start.10) | collective-permute-done | bytes 4194336 | tf_op jit(solution)/shard_map/ppermute | solution.py:14
  378.4 89.4 %while.62 = (s32[]{:T(128)}, f32[32,128,128]{2,1,0:T(8,128)}, s32[3,256]{1,0:T(4,128)S(1)}, s32[2,128]{1,0:T(2,128)}, s32[2,32]{1,0:T(2,128)}, /*index=5*/s32[]{...) while((s32[]{:T(128)}, f32[32,128,128]{2,1,0:T(8,128)}, ...), condition=%wide.region_12.13_spmd, body=%wide.region_10.12_spmd.sunk | while | flops 539496192 | bytes 67202240 | solution.py:58
  388.3 8.0 %fusion.55 = f32[128,128,128]{2,1,0:T(8,128)} fusion(bf16[128,128,128]{2,1,0:T(8,128)(2,1)} %gather_fusion.10, bf16[128,128,128]{2,1,0:T(8,128)(2,1)} %gather_fusion.11), kind=kOutput, calls=%fused_computation.113.clone.1 | convolution fusion | flops 536870912 | bytes 16777216 | tf_op jit(solution)/shard_map/while/body/eval_jaxpr/pij,pjk->pik/dot_general | solution.py:47
  403.0 17.1 %scatter_fusion.1 = f32[33,128,128]{2,1,0:T(8,128)S(1)} fusion(f32[33,128,128]{2,1,0:T(8,128)S(1)} %broadcast.704, s32[128]{0:T(128)S(1)} %fusion.54, f32[128,128,128]{2,1,0:T(8,128)} %fusion.55), kind=kCustom, calls=%fused_computation.26.clone.1 | custom fusion | flops 2097152 | bytes 25166336 | tf_op jit(solution)/shard_map/while/body/eval_jaxpr/scatter-add | solution.py:54
  432.9 8.0 %fusion.55 = f32[128,128,128]{2,1,0:T(8,128)} fusion(bf16[128,128,128]{2,1,0:T(8,128)(2,1)} %gather_fusion.10, bf16[128,128,128]{2,1,0:T(8,128)(2,1)} %gather_fusion.11), kind=kOutput, calls=%fused_computation.113.clone.1 | convolution fusion | flops 536870912 | bytes 16777216 | tf_op jit(solution)/shard_map/while/body/eval_jaxpr/pij,pjk->pik/dot_general | solution.py:47
  447.6 17.0 %scatter_fusion.1 = f32[33,128,128]{2,1,0:T(8,128)S(1)} fusion(f32[33,128,128]{2,1,0:T(8,128)S(1)} %broadcast.704, s32[128]{0:T(128)S(1)} %fusion.54, f32[128,128,128]{2,1,0:T(8,128)} %fusion.55), kind=kCustom, calls=%fused_computation.26.clone.1 | custom fusion | flops 2097152 | bytes 25166336 | tf_op jit(solution)/shard_map/while/body/eval_jaxpr/scatter-add | solution.py:54
  469.8 88.8 %while.63 = (s32[]{:T(128)}, f32[32,128,128]{2,1,0:T(8,128)}, s32[3,256]{1,0:T(4,128)S(1)}, s32[2,128]{1,0:T(2,128)}, s32[2,32]{1,0:T(2,128)}, /*index=5*/s32[]{...) while((s32[]{:T(128)}, f32[32,128,128]{2,1,0:T(8,128)}, ...), condition=%wide.region_15.16_spmd, body=%wide.region_13.15_spmd.sunk | while | flops 539496192 | bytes 67202240 | solution.py:58
  479.4 8.0 %fusion.60 = f32[128,128,128]{2,1,0:T(8,128)} fusion(bf16[128,128,128]{2,1,0:T(8,128)(2,1)} %gather_fusion.16, bf16[128,128,128]{2,1,0:T(8,128)(2,1)} %gather_fusion.17), kind=kOutput, calls=%fused_computation.114.clone.1 | convolution fusion | flops 536870912 | bytes 16777216 | tf_op jit(solution)/shard_map/while/body/eval_jaxpr/pij,pjk->pik/dot_general | solution.py:47
  494.0 17.1 %scatter_fusion.2 = f32[33,128,128]{2,1,0:T(8,128)S(1)} fusion(f32[33,128,128]{2,1,0:T(8,128)S(1)} %broadcast.712, s32[128]{0:T(128)S(1)} %fusion.59, f32[128,128,128]{2,1,0:T(8,128)} %fusion.60), kind=kCustom, calls=%fused_computation.27.clone.1 | custom fusion | flops 2097152 | bytes 25166336 | tf_op jit(solution)/shard_map/while/body/eval_jaxpr/scatter-add | solution.py:54
  523.8 8.0 %fusion.60 = f32[128,128,128]{2,1,0:T(8,128)} fusion(bf16[128,128,128]{2,1,0:T(8,128)(2,1)} %gather_fusion.16, bf16[128,128,128]{2,1,0:T(8,128)(2,1)} %gather_fusion.17), kind=kOutput, calls=%fused_computation.114.clone.1 | convolution fusion | flops 536870912 | bytes 16777216 | tf_op jit(solution)/shard_map/while/body/eval_jaxpr/pij,pjk->pik/dot_general | solution.py:47
  538.4 17.0 %scatter_fusion.2 = f32[33,128,128]{2,1,0:T(8,128)S(1)} fusion(f32[33,128,128]{2,1,0:T(8,128)S(1)} %broadcast.712, s32[128]{0:T(128)S(1)} %fusion.59, f32[128,128,128]{2,1,0:T(8,128)} %fusion.60), kind=kCustom, calls=%fused_computation.27.clone.1 | custom fusion | flops 2097152 | bytes 25166336 | tf_op jit(solution)/shard_map/while/body/eval_jaxpr/scatter-add | solution.py:54
  (186 shorter events, 187.4 us)
Async XLA Ops:
  3.3 10.0 %copy-start.7 = (s32[1,1,3,64]{3,1,2,0:T(1,128)S(1)}, s32[1,1,3,64]{3,1,2,0:T(1,128)}, u32[]{:S(2)}) copy-start(s32[1,1,3,64]{3,1,2,0:T(1,128)} %param.18) | copy-start | bytes 2308
  3.3 10.7 %copy-start.9 = (s32[1,1,3,32]{3,1,2,0:T(1,128)S(1)}, s32[1,1,3,32]{3,1,2,0:T(1,128)}, u32[]{:S(2)}) copy-start(s32[1,1,3,32]{3,1,2,0:T(1,128)} %param.20) | copy-start | bytes 1156
  3.3 10.7 %copy-start.8 = (s32[1,1,4,3,256]{4,2,3,1,0:T(4,128)S(1)}, s32[1,1,4,3,256]{4,2,3,1,0:T(4,128)}, u32[]{:S(2)}) copy-start(s32[1,1,4,3,256]{4,2,3,1,0:T(4,128)} %param.21) | copy-start | bytes 36868
  3.3 4.5 collective-permute-start.2
  3.3 10.8 %collective-permute-start.7 = (bf16[32,128,128]{2,1,0:T(8,128)(2,1)S(1)}, bf16[32,128,128]{2,1,0:T(8,128)(2,1)S(1)}, u32[]{:S(2)}, u32[]{:S(2)}) collective-permute-start(bf16[32,128,128]{2,1,0:T(8,128)(2,1)S(1)} %bitcast.251), channel_id=1, source_target_pairs={{0,4},{4,0},{8,12},{12,8},{16,20},{20,16},{24,28},{28,24},{1,5},{5... | collective-permute-start | bytes 3145736 | tf_op jit(solution)/shard_map/ppermute | solution.py:14
  11.0 84.0 %collective-permute-start.3 = (bf16[64,128,128]{2,1,0:T(8,128)(2,1)}, bf16[64,128,128]{2,1,0:T(8,128)(2,1)}, u32[]{:S(2)}, u32[]{:S(2)}) collective-permute-start(bf16[64,128,128]{2,1,0:T(8,128)(2,1)} %broadcast_select_fusion.1), channel_id=1, source_target_pairs={{0,8},{4,12},{8,0},{12,4},{16,24},{20,28},{24,16},{28,20},{1,9},{5... | collective-permute-start | bytes 6291464 | tf_op jit(solution)/shard_map/ppermute | solution.py:14
  13.3 1.5 collective-permute-start
  14.0 75.3 %collective-permute-start.5 = (s32[2,32]{1,0:T(2,128)S(1)}, s32[2,32]{1,0:T(2,128)S(1)}, u32[]{:S(2)}, u32[]{:S(2)}) collective-permute-start(s32[2,32]{1,0:T(2,128)S(1)} %bitcast.259), channel_id=1, source_target_pairs={{0,4},{4,0},{8,12},{12,8},{16,20},{20,16},{24,28},{28,24},{1,5},{5... | collective-permute-start | bytes 776 | tf_op jit(solution)/shard_map/ppermute | solution.py:14
  14.1 80.6 %collective-permute-start.11 = (bf16[32,128,128]{2,1,0:T(8,128)(2,1)S(1)}, bf16[32,128,128]{2,1,0:T(8,128)(2,1)}, u32[]{:S(2)}, u32[]{:S(2)}) collective-permute-start(bf16[32,128,128]{2,1,0:T(8,128)(2,1)S(1)} %collective-permute-done.7), channel_id=1, source_target_pairs={{0,8},{4,12},{8,0},{12,4},{16,24},{20,28},{24,16},{28,20},{1,9},{5... | collective-permute-start | bytes 3145736 | tf_op jit(solution)/shard_map/ppermute | solution.py:14
  14.8 67.0 %collective-permute-start.1 = (s32[3,64]{1,0:T(4,128)S(1)}, s32[3,64]{1,0:T(4,128)S(1)}, u32[]{:S(2)}, u32[]{:S(2)}) collective-permute-start(s32[3,64]{1,0:T(4,128)S(1)} %broadcast_select_fusion.2), channel_id=1, source_target_pairs={{0,8},{4,12},{8,0},{12,4},{16,24},{20,28},{24,16},{28,20},{1,9},{5... | collective-permute-start | bytes 2312 | tf_op jit(solution)/shard_map/ppermute | solution.py:14
  81.9 5.1 collective-permute-start.4
  87.0 8.0 %copy-start.5 = (s32[2,128]{1,0:T(2,128)}, s32[2,128]{1,0:T(2,128)S(1)}, u32[]{:S(2)}) copy-start(s32[2,128]{1,0:T(2,128)S(1)} %collective-permute-done.4) | copy-start | bytes 3076
  87.0 7.6 %collective-permute-start.8 = (s32[2,128]{1,0:T(2,128)S(1)}, s32[2,128]{1,0:T(2,128)}, u32[]{:S(2)}, u32[]{:S(2)}) collective-permute-start(s32[2,128]{1,0:T(2,128)S(1)} %collective-permute-done.4), channel_id=1, source_target_pairs={{0,2},{1,3},{2,0},{3,1},{4,6},{5,7},{6,4},{7,5},{8,10},{9,11},{10,... | collective-permute-start | bytes 3080 | tf_op jit(solution)/shard_map/ppermute | solution.py:14
  89.3 2.5 collective-permute-start.9
  91.8 376.0 %collective-permute-start.13 = (s32[2,32]{1,0:T(2,128)}, s32[2,32]{1,0:T(2,128)}, u32[]{:S(2)}, u32[]{:S(2)}) collective-permute-start(s32[2,32]{1,0:T(2,128)} %collective-permute-done.9), channel_id=1, source_target_pairs={{0,4},{4,0},{8,12},{12,8},{16,20},{20,16},{24,28},{28,24},{1,5},{5... | collective-permute-start | bytes 776 | tf_op jit(solution)/shard_map/ppermute | solution.py:14
  94.6 373.2 %collective-permute-start.12 = (s32[2,128]{1,0:T(2,128)}, s32[2,128]{1,0:T(2,128)}, u32[]{:S(2)}, u32[]{:S(2)}) collective-permute-start(s32[2,128]{1,0:T(2,128)} %collective-permute-done.8), channel_id=1, source_target_pairs={{0,1},{1,0},{2,3},{3,2},{4,5},{5,4},{6,7},{7,6},{8,9},{9,8},{10,11... | collective-permute-start | bytes 3080 | tf_op jit(solution)/shard_map/ppermute | solution.py:14
  94.7 373.1 %collective-permute-start.15 = (bf16[32,128,128]{2,1,0:T(8,128)(2,1)}, bf16[32,128,128]{2,1,0:T(8,128)(2,1)}, u32[]{:S(2)}, u32[]{:S(2)}) collective-permute-start(bf16[32,128,128]{2,1,0:T(8,128)(2,1)} %collective-permute-done.11), channel_id=1, source_target_pairs={{0,4},{4,0},{8,12},{12,8},{16,20},{20,16},{24,28},{28,24},{1,5},{5... | collective-permute-start | bytes 3145736 | tf_op jit(solution)/shard_map/ppermute | solution.py:14
  103.1 92.2 %collective-permute-start.6 = (bf16[128,128,128]{2,1,0:T(8,128)(2,1)}, bf16[128,128,128]{2,1,0:T(8,128)(2,1)}, u32[]{:S(2)}, u32[]{:S(2)}) collective-permute-start(bf16[128,128,128]{2,1,0:T(8,128)(2,1)} %constant_dynamic-update-slice_fusion), channel_id=1, source_target_pairs={{0,1},{1,0},{2,3},{3,2},{4,5},{5,4},{6,7},{7,6},{8,9},{9,8},{10,11... | collective-permute-start | bytes 12582920 | tf_op jit(solution)/shard_map/ppermute | solution.py:14
  104.5 90.8 %copy-start.6 = (s32[2,128]{1,0:T(2,128)S(1)}, s32[2,128]{1,0:T(2,128)}, u32[]{:S(2)}) copy-start(s32[2,128]{1,0:T(2,128)} %copy-done.5) | copy-start | bytes 3076
  195.3 183.1 %collective-permute-start.10 = (bf16[128,128,128]{2,1,0:T(8,128)(2,1)}, bf16[128,128,128]{2,1,0:T(8,128)(2,1)}, u32[]{:S(2)}, u32[]{:S(2)}) collective-permute-start(bf16[128,128,128]{2,1,0:T(8,128)(2,1)} %collective-permute-done.6), channel_id=1, source_target_pairs={{0,2},{1,3},{2,0},{3,1},{4,6},{5,7},{6,4},{7,5},{8,10},{9,11},{10,... | collective-permute-start | bytes 12582920 | tf_op jit(solution)/shard_map/ppermute | solution.py:14
  195.3 183.1 %copy-start.4 = (s32[1,1,1,3,256]{4,3,2,1,0:T(4,128)S(1)}, s32[1,1,1,3,256]{4,3,2,1,0:T(4,128)}, u32[]{:S(2)}) copy-start(s32[1,1,1,3,256]{4,3,2,1,0:T(4,128)} %copy.45) | copy-start | bytes 9220
  195.4 5.3 copy-start.2
  378.4 91.4 %collective-permute-start.14 = (bf16[128,128,128]{2,1,0:T(8,128)(2,1)}, bf16[128,128,128]{2,1,0:T(8,128)(2,1)}, u32[]{:S(2)}, u32[]{:S(2)}) collective-permute-start(bf16[128,128,128]{2,1,0:T(8,128)(2,1)} %collective-permute-done.10), channel_id=1, source_target_pairs={{0,1},{1,0},{2,3},{3,2},{4,5},{5,4},{6,7},{7,6},{8,9},{9,8},{10,11... | collective-permute-start | bytes 12582920 | tf_op jit(solution)/shard_map/ppermute | solution.py:14
  378.4 91.4 %copy-start.3 = (s32[1,1,1,3,256]{4,3,2,1,0:T(4,128)S(1)}, s32[1,1,1,3,256]{4,3,2,1,0:T(4,128)}, u32[]{:S(2)}) copy-start(s32[1,1,1,3,256]{4,3,2,1,0:T(4,128)} %copy.44) | copy-start | bytes 9220
  (3 other events, 10.2 us)
where the time goes:
time: 568 us; the launch traced here: 563 us
  waiting for transfers between devices  180 us (32%)
  other arithmetic  169 us (30%)
  local copies, waits for them, and re-layouts  134 us (24%)
  matrix products  64.1 us (11%)
  starting transfers between devices  14.4 us (3%)
    ppermute x16, waiting for transfers between devices, swapped(): return lax.ppermute(value, axis, pairs)  180 us
    scatter-add x8, other arithmetic, add_group(): jax.ops.segment_sum(blocks, target, num_segments=cell_count + 1)  136 us
    dot_general x8, matrix products, add_group(): jnp.einsum('pij,pjk->pik', left_all[left_slot], right_all[right_slot], pr...  64.1 us
    gather x8, local copies, waits for them, and re-layouts, add_group(): left_all[left_slot]  42.2 us
    gather x8, local copies, waits for them, and re-layouts, add_group(): right_all[right_slot]  29.7 us
    add x8, other arithmetic, add_group(): running + jax.ops.segment_sum(blocks, target, num_segments=cell_count + 1...  24.2 us
    gather x16, local copies, waits for them, and re-layouts, add_group(): weights = pair_group[2] * left_ids[1][left_slot] * right_ids[1][right_slot]  19.6 us
    ppermute x16, starting transfers between devices, swapped(): return lax.ppermute(value, axis, pairs)  14.4 us
  transfers between devices with their start and end apart: 16, of which 7 were waited for; matrix products, arithmetic and copies ran while one was open for 48% of the time, Pallas kernels for 0%

commit v1 on v0

v1 whole, which is shorter than its diff:
```python
import functools

import jax
import jax.numpy as jnp
from jax import lax
from jax.experimental import pallas as pl
from jax.experimental.pallas import tpu as pltpu
from jax.sharding import PartitionSpec as P

PANEL = 16
SLAB = 2
STEPS = 4
CHUNKS = 4
MESH = pl.DeviceIdType.MESH


def flipped(value, mask, bits):
    out = value
    for b in range(bits):
        w = 2**b
        out = out + ((mask // w) % 2) * (w - 2 * w * ((value // w) % 2))
    return out


def gather_kernel(
    stride, bits, own, slab, ids, row_all, pair_all, slab_all, row_ids, pair_ids, slab_ids,
    z_send, z_recv, p_send, p_recv, b_send, b_recv, l_sem,
):
    r = lax.axis_index("row")
    c = lax.axis_index("col")
    pos = c // stride
    rem = c % stride
    left = c - stride
    right = c + stride
    size = own.shape[0] // CHUNKS

    def partner(s):
        return flipped(r, s * stride + rem, bits)

    def shifted(t):
        return flipped(r, t * stride, bits)

    bar = pltpu.get_barrier_semaphore()

    def greet(row, col):
        pl.semaphore_signal(bar, inc=1, device_id=(row, col), device_id_type=MESH)

    def cond_kind(s):
        return s * stride + rem > 0

    @pl.when(pos > 0)
    def _():
        greet(r, left)

    @pl.when(pos < STEPS - 1)
    def _():
        greet(r, right)

    for s in range(STEPS):
        @pl.when(cond_kind(s))
        def _():
            greet(partner(s), c)
    for t in range(1, STEPS):
        greet(shifted(t), c)

    ends = jnp.minimum(pos, 1) + jnp.minimum(STEPS - 1 - pos, 1)
    pl.semaphore_wait(bar, ends + jnp.minimum(rem, 1) + 2 * (STEPS - 1))

    def piece(ref, id_ref, ch):
        return id_ref if ch == 0 else ref.at[pl.ds((ch - 1) * size, size)]

    def landed(s, ch):
        return row_ids.at[s] if ch == 0 else row_all.at[s, pl.ds((ch - 1) * size, size)]

    def paired(s, ch):
        return pair_ids.at[s] if ch == 0 else pair_all.at[s, pl.ds((ch - 1) * size, size)]

    def along(src, s, ch, way):
        return pltpu.make_async_remote_copy(
            src_ref=src, dst_ref=landed(s, ch), send_sem=z_send.at[way, s, ch],
            recv_sem=z_recv.at[s, ch], device_id=(r, right if way else left), device_id_type=MESH)

    def across(src, s, ch):
        return pltpu.make_async_remote_copy(
            src_ref=src, dst_ref=paired(s, ch), send_sem=p_send.at[s, ch],
            recv_sem=p_recv.at[s, ch], device_id=(partner(s), c), device_id_type=MESH)

    def slab_copy(src, t, to, what):
        dst = slab_ids.at[t] if what == 0 else slab_all.at[t]
        return pltpu.make_async_remote_copy(
            src_ref=src, dst_ref=dst, send_sem=b_send.at[t, what],
            recv_sem=b_recv.at[t, what], device_id=(shifted(to), c), device_id_type=MESH)

    pieces = range(CHUNKS + 1)
    for ch in pieces:
        mine = piece(own, ids, ch)

        @pl.when(pos > 0)
        def _():
            along(mine, pos, ch, 0).start()

        @pl.when(pos < STEPS - 1)
        def _():
            along(mine, pos, ch, 1).start()

        @pl.when(cond_kind(pos))
        def _():
            across(mine, pos, ch).start()
        if ch == 0:
            for what, src in ((0, ids), (1, slab)):
                slab_copy(src, 2, 2, what).start()
                slab_copy(src, 1, 1, what).start()
    local = (
        pltpu.make_async_copy(own, row_all.at[pos], l_sem.at[0]),
        pltpu.make_async_copy(ids, row_ids.at[pos], l_sem.at[1]),
        pltpu.make_async_copy(slab, slab_all.at[0], l_sem.at[2]),
        pltpu.make_async_copy(ids, slab_ids.at[0], l_sem.at[3]),
    )
    for copy in local:
        copy.start()

    for d in range(1, STEPS):
        for ch in pieces:
            for way in (1, 0):
                s = pos - d if way else pos + d
                here = s >= 0 if way else s <= STEPS - 1
                more = pos < STEPS - 1 if way else pos > 0

                @pl.when(here)
                def _():
                    along(landed(s, ch), s, ch, way).wait_recv()

                    @pl.when(more)
                    def _():
                        along(landed(s, ch), s, ch, way).start()

                    @pl.when(cond_kind(s))
                    def _():
                        across(landed(s, ch), s, ch).start()
            if d == 1 and ch == 1:
                for what, src in ((0, slab_ids.at[2]), (1, slab_all.at[2])):
                    slab_copy(src, 2, 2, what).wait_recv()
                    slab_copy(src, 3, 1, what).start()

    for what, src in ((0, ids), (1, slab)):
        slab_copy(src, 1, 1, what).wait()
        slab_copy(src, 2, 2, what).wait_send()
        slab_copy(src, 3, 1, what).wait()
    for s in range(STEPS):
        for ch in pieces:
            @pl.when(cond_kind(s))
            def _():
                across(landed(s, ch), s, ch).wait()

            @pl.when(jnp.logical_and(s <= pos, pos < STEPS - 1))
            def _():
                along(landed(s, ch), s, ch, 1).wait_send()

            @pl.when(jnp.logical_and(s >= pos, pos > 0))
            def _():
                along(landed(s, ch), s, ch, 0).wait_send()
    for copy in local:
        copy.wait()


def gather(own, slab, ids, stride, bits):
    any_spec = pl.BlockSpec(memory_space=pl.ANY)
    dma = pltpu.SemaphoreType.DMA
    return pl.pallas_call(
        functools.partial(gather_kernel, stride, bits),
        out_shape=(
            jax.ShapeDtypeStruct((STEPS,) + own.shape, own.dtype),
            jax.ShapeDtypeStruct((STEPS,) + own.shape, own.dtype),
            jax.ShapeDtypeStruct((STEPS,) + slab.shape, slab.dtype),
            jax.ShapeDtypeStruct((STEPS,) + ids.shape, ids.dtype),
            jax.ShapeDtypeStruct((STEPS,) + ids.shape, ids.dtype),
            jax.ShapeDtypeStruct((STEPS,) + ids.shape, ids.dtype),
        ),
        in_specs=[any_spec] * 3,
        out_specs=(any_spec,) * 6,
        scratch_shapes=[
            dma((2, STEPS, CHUNKS + 1)), dma((STEPS, CHUNKS + 1)),
            dma((STEPS, CHUNKS + 1)), dma((STEPS, CHUNKS + 1)),
            dma((STEPS, 2)), dma((STEPS, 2)), dma((4,)),
        ],
        compiler_params=pltpu.CompilerParams(collective_id=0, has_side_effects=True),
    )(own, slab, ids)


def product_kernel(info, row_ids, pair_ids, slab_ids, row_ref, pair_ref, slab_ref, out, dense, right, acc):
    step = pl.program_id(0)
    r, q_mask, c = info[0], info[4 + step], info[1]
    slab_at = info[8 + step]
    q = r ^ q_mask
    slots, edge = row_ref.shape[1], row_ref.shape[2]
    low = jnp.minimum(r, q) * PANEL
    high = jnp.maximum(r, q) * PANEL

    @pl.when(step == 0)
    def _():
        acc[...] = jnp.zeros_like(acc)

    dense[...] = jnp.zeros_like(dense)
    right[...] = jnp.zeros_like(right)

    def put_slab(h, carry):
        k = slab_ids[slab_at, 3, h] - q * PANEL
        k = jnp.where(slab_ids[slab_at, 5, h] > 0, k, PANEL)
        n = slab_ids[slab_at, 4, h] - c * SLAB
        n = jnp.where(slab_ids[slab_at, 5, h] > 0, n, 0)
        lane = pl.multiple_of(n * edge, edge)
        right[k, :, pl.ds(lane, edge)] = slab_ref[0, h]
        return carry

    lax.fori_loop(0, slab_ref.shape[1], put_slab, 0, unroll=4)

    def put(ids, ref, turn, drop):
        def body(h, carry):
            i = ids[step, 0, h] - low
            j = ids[step, 1, h] - high
            keep = ids[step, 2, h] > 0
            if drop:
                keep = jnp.logical_and(keep, i != j)
            at_row, at_col = (j, i) if turn else (i, j)
            at_row = jnp.where(keep, at_row, PANEL)
            at_col = jnp.where(keep, at_col, 0)
            lane = pl.multiple_of(at_col * edge, edge)
            block = ref[0, h]
            dense[at_row, :, pl.ds(lane, edge)] = block.T if turn else block
            return carry

        lax.fori_loop(0, slots, body, 0, unroll=4)

    @pl.when(r < q)
    def _():
        put(row_ids, row_ref, False, False)
        put(pair_ids, pair_ref, False, False)

    @pl.when(r > q)
    def _():
        put(row_ids, row_ref, True, False)
        put(pair_ids, pair_ref, True, False)

    @pl.when(r == q)
    def _():
        put(row_ids, row_ref, False, False)
        put(row_ids, row_ref, True, True)

    depth = PANEL * edge
    group = 2
    slab_full = right[:PANEL].reshape(depth, SLAB * edge)

    def rows(g, carry):
        lhs = dense[pl.ds(g * group, group)].reshape(group * edge, depth)
        at = pl.multiple_of(g * group * edge, group * edge)
        acc[pl.ds(at, group * edge)] += jnp.dot(lhs, slab_full, preferred_element_type=jnp.float32)
        return carry

    lax.fori_loop(0, PANEL // group, rows, 0)

    @pl.when(step == pl.num_programs(0) - 1)
    def _():
        out[...] = acc[...].astype(out.dtype)


def multiply(info, row_ids, pair_ids, slab_ids, row_all, pair_all, slab_all):
    slots, edge = row_all.shape[1], row_all.shape[2]
    held = (1, slots, edge, edge)
    return pl.pallas_call(
        product_kernel,
        grid_spec=pltpu.PrefetchScalarGridSpec(
            num_scalar_prefetch=4,
            grid=(STEPS,),
            in_specs=[
                pl.BlockSpec(held, lambda s, *_: (s, 0, 0, 0)),
                pl.BlockSpec(held, lambda s, *_: (s, 0, 0, 0)),
                pl.BlockSpec((1,) + slab_all.shape[1:], lambda s, info, *_: (info[8 + s], 0, 0, 0)),
            ],
            out_specs=pl.BlockSpec((PANEL * edge, SLAB * edge), lambda s, *_: (0, 0)),
            scratch_shapes=[
                pltpu.VMEM((PANEL + 1, edge, PANEL * edge), jnp.bfloat16),
                pltpu.VMEM((PANEL + 1, edge, SLAB * edge), jnp.bfloat16),
                pltpu.VMEM((PANEL * edge, SLAB * edge), jnp.float32),
            ],
        ),
        out_shape=jax.ShapeDtypeStruct((PANEL * edge, SLAB * edge), jnp.bfloat16),
        compiler_params=pltpu.CompilerParams(vmem_limit_bytes=50 * 2**20),
    )(info, row_ids, pair_ids, slab_ids, row_all, pair_all, slab_all)


def on_device(stored_blocks, stored_ids, slab_blocks, slab_ids, pair_lists):
    r = lax.axis_index("row")
    c = lax.axis_index("col")
    stride = lax.axis_size("col") // STEPS
    bits = lax.axis_size("row").bit_length() - 1
    ids = jnp.concatenate(
        [
            jnp.pad(stored_ids[0, 0], ((0, 0), (0, 128 - stored_ids.shape[-1]))),
            jnp.pad(slab_ids[0, 0], ((0, 2), (0, 128 - slab_ids.shape[-1]))),
        ]
    )
    row_all, pair_all, slab_all, row_i, pair_i, slab_i = gather(
        stored_blocks[0, 0], slab_blocks[0, 0], ids, stride, bits
    )
    pos = c // stride
    steps = jnp.arange(STEPS, dtype=jnp.int32)
    zero = jnp.zeros((2,), jnp.int32)
    info = jnp.concatenate(
        [jnp.stack([r, c]).astype(jnp.int32), zero, steps * stride + c % stride, steps ^ pos]
    )
    return multiply(info, row_i, pair_i, slab_i, row_all, pair_all, slab_all)


def solution(mesh):
    return jax.shard_map(
        on_device,
        mesh=mesh,
        in_specs=(
            P("row", "col", None, None, None),
            P("row", "col", None, None),
            P("row", "col", None, None, None),
            P("row", "col", None, None),
            P("row", "col", None, None, None),
        ),
        out_specs=P("row", "col"),
        check_vma=False,
    )
```

time: 568 us -> 193 us (0.34)
  Pallas kernels: 0 us -> 185 us
  waiting for transfers between devices: 180 us -> 0 us
  other arithmetic: 169 us -> 0.61 us
  local copies, waits for them, and re-layouts: 134 us -> 3.6 us
  matrix products: 64.1 us -> 0 us
  starting transfers between devices: 14.4 us -> 0 us
    pallas_call x0 -> x2, Pallas kernels: none -> 185 us  [the longest x1 154 us: gather(): pl.pallas_call(functools.partial(gather_kernel, stride, bits), out_shape=...]
    ppermute x16 -> x0, waiting for transfers between devices: 180 us -> none  [swapped(): return lax.ppermute(value, axis, pairs)]
    scatter-add x8 -> x0, other arithmetic: 136 us -> none  [add_group(): jax.ops.segment_sum(blocks, target, num_segments=cell_count + 1)]
    gather x48 -> x0, local copies, waits for them, and re-layouts: 111 us -> none  [the longest x8 42.2 us: add_group(): left_all[left_slot]]
    dot_general x8 -> x0, matrix products: 64.1 us -> none  [add_group(): jnp.einsum('pij,pjk->pik', left_all[left_slot], right_all[right_slot], pr...]
    add x8 -> x0, other arithmetic: 24.2 us -> none  [add_group(): running + jax.ops.segment_sum(blocks, target, num_segments=cell_count + 1...]
    ppermute x16 -> x0, starting transfers between devices: 14.4 us -> none  [swapped(): return lax.ppermute(value, axis, pairs)]
    squeeze x16 -> x0, local copies, waits for them, and re-layouts: 5.79 us -> none  [the longest x8 2.92 us: add_group(): left_ids[0][left_slot] - out_row * PANEL]
  transfers between devices with their start and end apart: 16 -> 0, of which waited for: 7 -> 0; matrix products, arithmetic and copies ran while one was open for 48% -> 0% of each run, Pallas kernels for 0% -> 0%
where the time goes in v1:
time: 193 us; the launch traced here: 190 us
  Pallas kernels  185 us (96%)
  local copies, waits for them, and re-layouts  3.6 us (2%)
    pallas_call x1, Pallas kernels, gather(): pl.pallas_call(functools.partial(gather_kernel, stride, bits), out_shape=...  154 us
    pallas_call x1, Pallas kernels, multiply(): pl.pallas_call(product_kernel, grid_spec=pltpu.PrefetchScalarGridSpec(num...  31.7 us

profile of v1, /device:TPU:1, one launch (start us, length us, event | category | flops | bytes accessed | tf_op | source)
XLA Modules:
  0.0 189.6 jit_solution(3120717822966924360)
XLA Ops:
  0.0 0.1 concatenate.6.info
  0.1 0.7 copy.10
  0.8 0.7 copy.9
  1.5 0.6 pad_add_fusion.ids
  2.1 153.7 %shard_map.46 = (bf16[4,64,128,128]{3,2,1,0:T(8,128)(2,1)}, bf16[4,64,128,128]{3,2,1,0:T(8,128)(2,1)}, bf16[4,32,128,128]{3,2,1,0:T(8,128)(2,1)}, s32[4,8,128]{2...) custom-call(bf16[64,128,128]{2,1,0:T(8,128)(2,1)} %bitcast.10, bf16[32,128,128]{2,1,0:T(8,128)(2,1)} %bitcast.11, ...), custom_call_target="tpu_custom_call" | custom-call | tf_op jit(solution)/shard_map/pallas_call | solution.py:169
  155.8 0.0 copy-start
  155.8 0.7 copy-done
  156.5 0.0 copy-start.1
  156.5 0.7 copy-done.1
  157.2 0.0 copy-start.2
  157.2 0.7 copy-done.2
  157.9 31.7 %shard_map.47 = bf16[2048,256]{1,0:T(8,128)(2,1)} custom-call(s32[12]{0:T(128)S(1)} %concatenate.6.info, s32[4,8,128]{2,1,0:T(8,128)S(1)} %copy-done, s32[4,8,128]{2,1,0:T(8,128)S(1)} %copy-done.1, s32[4,8,128]{2,1,0:T(8,128)S(1)} %copy-done.2, bf16[4,64,128,128]{3,2,1,0:T(8,128)(2,1)} %get-tuple-element.14.row_ref, ...), custom_call_target="tpu_custom_call" | custom-call | tf_op jit(solution)/shard_map/pallas_call | solution.py:269
  (3 shorter events, 0.0 us)
Async XLA Ops:
  155.8 0.7 copy-start
  156.5 0.7 copy-start.1
  157.2 0.7 copy-start.2

commit v2 on v1

v2 whole, which is shorter than its diff:
```python
import functools

import jax
import jax.numpy as jnp
from jax import lax
from jax.experimental import pallas as pl
from jax.experimental.pallas import tpu as pltpu
from jax.sharding import PartitionSpec as P

PANEL = 16
SLAB = 2
STEPS = 4
CHUNKS = 4
MESH = pl.DeviceIdType.MESH


def flipped(value, mask, bits):
    out = value
    for b in range(bits):
        w = 2**b
        out = out + ((mask // w) % 2) * (w - 2 * w * ((value // w) % 2))
    return out


def gather_kernel(
    stride, bits, own, slab, ids, out, blocks, slabs, row_ids, pair_ids, slab_ids,
    stage, dense, right_all, acc, table, scalars,
    z_send, z_recv, p_send, p_recv, b_send, b_recv, l_sem, t_sem,
):
    r = lax.axis_index("row")
    c = lax.axis_index("col")
    pos = c // stride
    rem = c % stride
    left = c - stride
    right = c + stride
    slots, edge = own.shape[0], own.shape[1]
    size = slots // CHUNKS
    slab_slots = slab.shape[0]

    def partner(s):
        return flipped(r, s * stride + rem, bits)

    def shifted(t):
        return flipped(r, t * stride, bits)

    bar = pltpu.get_barrier_semaphore()

    def greet(row, col):
        pl.semaphore_signal(bar, inc=1, device_id=(row, col), device_id_type=MESH)

    def cond_kind(s):
        return s * stride + rem > 0

    @pl.when(pos > 0)
    def _():
        greet(r, left)

    @pl.when(pos < STEPS - 1)
    def _():
        greet(r, right)

    for s in range(STEPS):
        @pl.when(cond_kind(s))
        def _():
            greet(partner(s), c)
    for t in range(1, STEPS):
        greet(shifted(t), c)

    ends = jnp.minimum(pos, 1) + jnp.minimum(STEPS - 1 - pos, 1)
    pl.semaphore_wait(bar, ends + jnp.minimum(rem, 1) + 2 * (STEPS - 1))

    def piece(ref, id_ref, ch):
        return id_ref if ch == 0 else ref.at[pl.ds((ch - 1) * size, size)]

    def landed(s, ch):
        return row_ids.at[s] if ch == 0 else blocks.at[s, pl.ds(1 + (ch - 1) * size, size)]

    def paired(s, ch):
        return pair_ids.at[s] if ch == 0 else blocks.at[s, pl.ds(1 + slots + (ch - 1) * size, size)]

    def along(src, s, ch, way):
        return pltpu.make_async_remote_copy(
            src_ref=src, dst_ref=landed(s, ch), send_sem=z_send.at[way, s, ch],
            recv_sem=z_recv.at[s, ch], device_id=(r, right if way else left), device_id_type=MESH)

    def across(src, s, ch):
        return pltpu.make_async_remote_copy(
            src_ref=src, dst_ref=paired(s, ch), send_sem=p_send.at[s, ch],
            recv_sem=p_recv.at[s, ch], device_id=(partner(s), c), device_id_type=MESH)

    def slab_copy(src, t, to, what):
        dst = slab_ids.at[t] if what == 0 else slabs.at[t, pl.ds(1, slab_slots)]
        return pltpu.make_async_remote_copy(
            src_ref=src, dst_ref=dst, send_sem=b_send.at[t, what],
            recv_sem=b_recv.at[t, what], device_id=(shifted(to), c), device_id_type=MESH)

    pieces = range(CHUNKS + 1)
    for ch in pieces:
        mine = piece(own, ids, ch)

        @pl.when(pos > 0)
        def _():
            along(mine, pos, ch, 0).start()

        @pl.when(pos < STEPS - 1)
        def _():
            along(mine, pos, ch, 1).start()

        @pl.when(cond_kind(pos))
        def _():
            across(mine, pos, ch).start()
        if ch == 0:
            for what, src in ((0, ids), (1, slab)):
                slab_copy(src, 2, 2, what).start()
                slab_copy(src, 1, 1, what).start()
    local = (
        pltpu.make_async_copy(own, blocks.at[pos, pl.ds(1, slots)], l_sem.at[0]),
        pltpu.make_async_copy(ids, row_ids.at[pos], l_sem.at[1]),
        pltpu.make_async_copy(slab, slabs.at[0, pl.ds(1, slab_slots)], l_sem.at[2]),
        pltpu.make_async_copy(ids, slab_ids.at[0], l_sem.at[3]),
    )
    for copy in local:
        copy.start()

    zero_block = jnp.zeros((edge, edge), blocks.dtype)
    stage[0] = zero_block
    for s in range(STEPS):
        slabs[s, 0] = zero_block
    acc[...] = jnp.zeros_like(acc)
    sub = lax.broadcasted_iota(jnp.int32, (PANEL, 128), 0)
    lane = lax.broadcasted_iota(jnp.int32, (PANEL, 128), 1)

    def inverted(at_row, at_col, present, base, rows):
        value = jnp.where(present, lane[:1] + (1 + base), 0)
        hit = jnp.where(at_col == sub, value, 0)
        found = jnp.zeros((PANEL, 128), jnp.int32)
        for a in range(rows):
            most = jnp.max(jnp.where(at_row == a, hit, 0), axis=1, keepdims=True)
            found = jnp.where(lane == a, most, found)
        return found

    def process(s):
        q = partner(s)
        low, high = jnp.minimum(r, q) * PANEL, jnp.maximum(r, q) * PANEL
        t = flipped(s, pos, 2)

        def part(ref, base, turn):
            i, j = ref[s, 0:1] - low, ref[s, 1:2] - high
            keep = ref[s, 2:3] > 0
            return inverted(j if turn else i, i if turn else j, keep, base, PANEL)

        @pl.when(r < q)
        def _():
            table[0:PANEL] = jnp.maximum(part(row_ids, 0, False), part(pair_ids, slots, False))

        @pl.when(r > q)
        def _():
            table[0:PANEL] = jnp.maximum(part(row_ids, 0, True), part(pair_ids, slots, True))

        @pl.when(r == q)
        def _():
            i, j = row_ids[s, 0:1] - low, row_ids[s, 1:2] - high
            keep = row_ids[s, 2:3] > 0
            off = jnp.logical_and(keep, i != j)
            table[0:PANEL] = jnp.maximum(
                inverted(i, j, keep, 0, PANEL), inverted(j, i, off, slots, PANEL))

        table[PANEL:] = inverted(
            slab_ids[t, 4:5] - c * SLAB, slab_ids[t, 3:4] - q * PANEL, slab_ids[t, 5:6] > 0, 0, SLAB)
        fetch = pltpu.make_async_copy(table, scalars, t_sem.at[0])
        fetch.start()
        fetch.wait()

        def slab_row(k, carry):
            for n in range(SLAB):
                right_all[k, :, n * edge : (n + 1) * edge] = slabs[t, scalars[PANEL + k, n]]
            return carry

        lax.fori_loop(0, PANEL, slab_row, 0)

        def hold(to, of, count, turn):
            def some(g, carry):
                for x in range(4):
                    block = blocks[s, of + g * 4 + x]
                    stage[to + g * 4 + x] = block.T if turn else block
                return carry

            lax.fori_loop(0, count // 4, some, 0)

        @pl.when(r < q)
        def _():
            hold(1, 1, 2 * slots, False)

        @pl.when(r > q)
        def _():
            hold(1, 1, 2 * slots, True)

        @pl.when(r == q)
        def _():
            hold(1, 1, slots, False)
            hold(1 + slots, 1, slots, True)

        def fill(i, carry):
            for j in range(PANEL):
                dense[i, :, j * edge : (j + 1) * edge] = stage[scalars[j, i]]
            return carry

        lax.fori_loop(0, PANEL, fill, 0)
        depth = PANEL * edge
        slab_full = right_all[...].reshape(depth, SLAB * edge)
        group = 2

        def product(g, carry):
            lhs = dense[pl.ds(g * group, group)].reshape(group * edge, depth)
            at = pl.multiple_of(g * group * edge, group * edge)
            acc[pl.ds(at, group * edge)] += jnp.dot(
                lhs, slab_full, preferred_element_type=jnp.float32)
            return carry

        lax.fori_loop(0, PANEL // group, product, 0)

    second = 1 + pos % 2
    last = (STEPS - 1) * (1 - pos // 2)
    third = 6 - pos - second - last

    def take(s):
        for ch in pieces:
            @pl.when(cond_kind(s))
            def _():
                across(landed(s, ch), s, ch).wait_recv()
        process(s)

    for d in range(1, STEPS):
        for ch in pieces:
            for way in (1, 0):
                s = pos - d if way else pos + d
                here = s >= 0 if way else s <= STEPS - 1
                more = pos < STEPS - 1 if way else pos > 0

                @pl.when(here)
                def _():
                    along(landed(s, ch), s, ch, way).wait_recv()

                    @pl.when(more)
                    def _():
                        along(landed(s, ch), s, ch, way).start()

                    @pl.when(cond_kind(s))
                    def _():
                        across(landed(s, ch), s, ch).start()
            if d == 1 and ch == 1:
                for what, src in ((0, slab_ids.at[2]), (1, slabs.at[2, pl.ds(1, slab_slots)])):
                    slab_copy(src, 2, 2, what).wait_recv()
                    slab_copy(src, 3, 1, what).start()

        if d == 1:
            for copy in local:
                copy.wait()
            for what, src in ((0, ids), (1, slab)):
                slab_copy(src, 1, 1, what).wait()
                slab_copy(src, 2, 2, what).wait_send()
                slab_copy(src, 3, 1, what).wait()
            take(pos)
        if d == 2:
            take(second)
            take(third)
    take(last)
    out[...] = acc[...].astype(out.dtype)
    for s in range(STEPS):
        for ch in pieces:
            @pl.when(cond_kind(s))
            def _():
                across(landed(s, ch), s, ch).wait_send()

            @pl.when(jnp.logical_and(s <= pos, pos < STEPS - 1))
            def _():
                along(landed(s, ch), s, ch, 1).wait_send()

            @pl.when(jnp.logical_and(s >= pos, pos > 0))
            def _():
                along(landed(s, ch), s, ch, 0).wait_send()


def gather(own, slab, ids, stride, bits):
    any_spec = pl.BlockSpec(memory_space=pl.ANY)
    dma = pltpu.SemaphoreType.DMA
    slots, edge = own.shape[0], own.shape[1]
    tile = (PANEL * edge, SLAB * edge)
    listed = pltpu.VMEM((STEPS,) + ids.shape, ids.dtype)
    return pl.pallas_call(
        functools.partial(gather_kernel, stride, bits),
        out_shape=jax.ShapeDtypeStruct(tile, own.dtype),
        in_specs=[any_spec] * 3,
        out_specs=pl.BlockSpec(memory_space=pltpu.VMEM),
        scratch_shapes=[
            pltpu.VMEM((STEPS, 2 * slots + 1, edge, edge), own.dtype),
            pltpu.VMEM((STEPS, slab.shape[0] + 1, edge, edge), own.dtype),
            listed, listed, listed,
            pltpu.VMEM((2 * slots + 1, edge, edge), own.dtype),
            pltpu.VMEM((PANEL, edge, PANEL * edge), own.dtype),
            pltpu.VMEM((PANEL, edge, SLAB * edge), own.dtype),
            pltpu.VMEM(tile, jnp.float32),
            pltpu.VMEM((2 * PANEL, 128), jnp.int32),
            pltpu.SMEM((2 * PANEL, 128), jnp.int32),
            dma((2, STEPS, CHUNKS + 1)), dma((STEPS, CHUNKS + 1)),
            dma((STEPS, CHUNKS + 1)), dma((STEPS, CHUNKS + 1)),
            dma((STEPS, 2)), dma((STEPS, 2)), dma((4,)), dma((1,)),
        ],
        compiler_params=pltpu.CompilerParams(
            collective_id=0, has_side_effects=True, vmem_limit_bytes=56 * 2**20
        ),
    )(own, slab, ids)


def on_device(stored_blocks, stored_ids, slab_blocks, slab_ids, pair_lists):
    stride = lax.axis_size("col") // STEPS
    bits = lax.axis_size("row").bit_length() - 1
    ids = jnp.concatenate(
        [
            jnp.pad(stored_ids[0, 0], ((0, 0), (0, 128 - stored_ids.shape[-1]))),
            jnp.pad(slab_ids[0, 0], ((0, 2), (0, 128 - slab_ids.shape[-1]))),
        ]
    )
    return gather(stored_blocks[0, 0], slab_blocks[0, 0], ids, stride, bits)


def solution(mesh):
    return jax.shard_map(
        on_device,
        mesh=mesh,
        in_specs=(
            P("row", "col", None, None, None),
            P("row", "col", None, None),
            P("row", "col", None, None, None),
            P("row", "col", None, None),
            P("row", "col", None, None, None),
        ),
        out_specs=P("row", "col"),
        check_vma=False,
    )
```

time: 193 us -> 178 us (0.922); the launches traced: 190 us -> 177 us
  Pallas kernels: 185 us -> 173 us
    pallas_call x1 -> x0, Pallas kernels: 31.7 us -> none  [multiply(): pl.pallas_call(product_kernel, grid_spec=pltpu.PrefetchScalarGridSpec(num...]
    pallas_call x1, Pallas kernels: 154 us -> 173 us  [gather(): pl.pallas_call(functools.partial(gather_kernel, stride, bits), out_shape=...]
where the time goes in v2:
time: 178 us; the launch traced here: 177 us
  Pallas kernels  173 us (97%)
  local copies, waits for them, and re-layouts  3.62 us (2%)
    pallas_call x1, Pallas kernels, gather(): pl.pallas_call(functools.partial(gather_kernel, stride, bits), out_shape=...  173 us
    unnamed x3, local copies, waits for them, and re-layouts  3.62 us

profile of v2, /device:TPU:1, one launch (start us, length us, event | category | flops | bytes accessed | tf_op | source)
XLA Modules:
  0.0 177.3 jit_solution(6293452063676925950)
XLA Ops:
  0.0 0.7 copy.10
  0.7 0.7 copy.9
  1.4 0.6 pad_add_fusion.ids
  2.0 173.1 %shard_map.46 = bf16[2048,256]{1,0:T(8,128)(2,1)} custom-call(bf16[64,128,128]{2,1,0:T(8,128)(2,1)} %bitcast.8, bf16[32,128,128]{2,1,0:T(8,128)(2,1)} %bitcast.9, s32[8,128]{1,0:T(8,128)} %pad_add_fusion.ids), custom_call_target="tpu_custom_call" | custom-call | tf_op jit(solution)/shard_map/pallas_call | solution.py:290
  175.1 2.3 %copy.12 = bf16[2048,256]{1,0:T(8,128)(2,1)} copy(bf16[2048,256]{1,0:T(8,128)(2,1)} %shard_map.46) | data formatting | bytes 2097152

commit v3 on v2

--- a/solution.py
+++ b/solution.py
@@ -10,7 +10,7 @@
 PANEL = 16
 SLAB = 2
 STEPS = 4
-CHUNKS = 4
+CHUNKS = 8
 MESH = pl.DeviceIdType.MESH
 
 
@@ -95,10 +95,11 @@
             recv_sem=b_recv.at[t, what], device_id=(shifted(to), c), device_id_type=MESH)
 
     pieces = range(CHUNKS + 1)
+    kept = 1 + CHUNKS // 2
     for ch in pieces:
         mine = piece(own, ids, ch)
 
-        @pl.when(pos > 0)
+        @pl.when(pos > (1 if ch >= kept else 0))
         def _():
             along(mine, pos, ch, 0).start()
 
@@ -219,8 +220,8 @@
 
         lax.fori_loop(0, PANEL // group, product, 0)
 
-    second = 1 + pos % 2
-    last = (STEPS - 1) * (1 - pos // 2)
+    second = jnp.where(pos == 2, 1, 2)
+    last = jnp.where(pos == 0, 1, jnp.where(pos == 1, 3, 0))
     third = 6 - pos - second - last
 
     def take(s):
@@ -235,6 +236,8 @@
             for way in (1, 0):
                 s = pos - d if way else pos + d
                 here = s >= 0 if way else s <= STEPS - 1
+                if d == 1 and not way and ch >= kept:
+                    here = jnp.logical_and(here, pos > 0)
                 more = pos < STEPS - 1 if way else pos > 0
 
                 @pl.when(here)
@@ -262,8 +265,20 @@
                 slab_copy(src, 3, 1, what).wait()
             take(pos)
         if d == 2:
+            @pl.when(pos == 1)
+            def _():
+                for ch in range(kept, CHUNKS + 1):
+                    along(piece(own, ids, ch), pos, ch, 0).start()
+
             take(second)
-            take(third)
+    take(third)
+
+    @pl.when(pos == 0)
+    def _():
+        for ch in range(kept, CHUNKS + 1):
+            along(landed(1, ch), 1, ch, 0).wait_recv()
+            across(landed(1, ch), 1, ch).start()
+
     take(last)
     out[...] = acc[...].astype(out.dtype)
     for s in range(STEPS):

time: 178 us -> 170 us (0.955)
  Pallas kernels: 173 us -> 166 us
    pallas_call x1, Pallas kernels: 173 us -> 166 us  [gather(): pl.pallas_call(functools.partial(gather_kernel, stride, bits), out_shape=...]
where the time goes in v3:
time: 170 us
  Pallas kernels  166 us (98%)
  local copies, waits for them, and re-layouts  3.62 us (2%)
    pallas_call x1, Pallas kernels, gather(): pl.pallas_call(functools.partial(gather_kernel, stride, bits), out_shape=...  166 us
    unnamed x3, local copies, waits for them, and re-layouts  3.62 us

profile of v3, /device:TPU:1, one launch (start us, length us, event | category | flops | bytes accessed | tf_op | source)
XLA Modules:
  0.0 169.8 jit_solution(8529146060261085254)
XLA Ops:
  0.0 0.7 copy.10
  0.7 0.7 copy.9
  1.4 0.6 pad_add_fusion.ids
  2.0 165.5 %shard_map.46 = bf16[2048,256]{1,0:T(8,128)(2,1)} custom-call(bf16[64,128,128]{2,1,0:T(8,128)(2,1)} %bitcast.8, bf16[32,128,128]{2,1,0:T(8,128)(2,1)} %bitcast.9, s32[8,128]{1,0:T(8,128)} %pad_add_fusion.ids), custom_call_target="tpu_custom_call" | custom-call | tf_op jit(solution)/shard_map/pallas_call | solution.py:305
  167.5 2.3 %copy.12 = bf16[2048,256]{1,0:T(8,128)(2,1)} copy(bf16[2048,256]{1,0:T(8,128)(2,1)} %shard_map.46) | data formatting | bytes 2097152

commit v4 on v3

--- a/solution.py
+++ b/solution.py
@@ -10,7 +10,7 @@
 PANEL = 16
 SLAB = 2
 STEPS = 4
-CHUNKS = 8
+CHUNKS = 4
 MESH = pl.DeviceIdType.MESH
 
 

time: 170 us -> 167 us (0.982)
  Pallas kernels: 166 us -> 162 us
    pallas_call x1, Pallas kernels: 166 us -> 162 us  [gather(): pl.pallas_call(functools.partial(gather_kernel, stride, bits), out_shape=...]
where the time goes in v4:
time: 167 us
  Pallas kernels  162 us (97%)
  local copies, waits for them, and re-layouts  3.62 us (2%)
    pallas_call x1, Pallas kernels, gather(): pl.pallas_call(functools.partial(gather_kernel, stride, bits), out_shape=...  162 us
    unnamed x3, local copies, waits for them, and re-layouts  3.62 us

profile of v4, /device:TPU:1, one launch (start us, length us, event | category | flops | bytes accessed | tf_op | source)
XLA Modules:
  0.0 166.7 jit_solution(14234175956978626109)
XLA Ops:
  0.0 0.7 copy.10
  0.7 0.7 copy.9
  1.4 0.6 pad_add_fusion.ids
  2.0 162.5 %shard_map.46 = bf16[2048,256]{1,0:T(8,128)(2,1)} custom-call(bf16[64,128,128]{2,1,0:T(8,128)(2,1)} %bitcast.8, bf16[32,128,128]{2,1,0:T(8,128)(2,1)} %bitcast.9, s32[8,128]{1,0:T(8,128)} %pad_add_fusion.ids), custom_call_target="tpu_custom_call" | custom-call | tf_op jit(solution)/shard_map/pallas_call | solution.py:305
  164.4 2.3 %copy.12 = bf16[2048,256]{1,0:T(8,128)(2,1)} copy(bf16[2048,256]{1,0:T(8,128)(2,1)} %shard_map.46) | data formatting | bytes 2097152
